TPU v7x, 128 devices: a whole 4x4x4 slice. The times are simulated.
128 devices in a mesh: row: 8 (over y, core), col: 16 (over z, x).
Axes of the slice: x: 4, y: 4, z: 4, core: 2. Of those that a mesh axis runs over, the one named last changes fastest.
Arguments:
- features: float32 [256, 1024, 128], P('row', 'col'), may hold values from -0.4 to 0.4
- step_size: float32 [256, 1024, 128], P('row', 'col'), may hold values from 0.5 to 2
- write_weights: float32 [256, 1024, 16], P('row', 'col'), may hold values from -6 to 6
- read_weights: float32 [256, 1024, 16], P('row', 'col'), may hold values from -6 to 6
- decay_log: float32 [16, 128], replicated, may hold values from -7.6 to -3.5
- out_grad: float32 [256, 1024, 128], P('row', 'col'), may hold values from -0.4 to 0.4
Outputs:
- grad_features: float32 [256, 1024, 128], P('row', 'col')
- grad_step: float32 [256, 1024, 128], P('row', 'col')
- grad_write: float32 [256, 1024, 16], P('row', 'col')
- grad_read: float32 [256, 1024, 16], P('row', 'col')
- grad_decay: float32 [16, 128], replicated
All inputs are finite; a program needn't handle non-finite values.
Results may differ from a plain program's by a relative error of at most 0.0002.
Values sent between devices are 32-bit elements; how exact they have to be, the bound alone decides.
A program may use at most 320 MiB of HBM per device.

v0:
```python
import jax
import jax.numpy as jnp
from jax import lax
from jax.sharding import PartitionSpec as P


def carried_in(shard, axis, combine, identity, reverse):
    size, mine = (lax.axis_size(axis), lax.axis_index(axis))
    everything = jax.tree.map(lambda part: lax.all_gather(part, axis), shard)
    start = jax.tree.map(
        lambda part, zero: jnp.broadcast_to(jnp.asarray(zero, part.dtype), part.shape),
        shard,
        identity,
    )

    def lap(k, before):
        at = size - 1 - k if reverse else k
        reached = at > mine if reverse else at < mine
        new = combine(before, jax.tree.map(lambda part: part[at], everything))
        return jax.tree.map(lambda a, b: jnp.where(reached, a, b), new, before)

    return lax.fori_loop(0, size, lap, start)


def sweep_rows(decays, driving, backward):

    def advance(current, inputs):
        factor, source = inputs
        current = factor * current + source
        return (current, current)

    def retreat(passed, inputs):
        factor, source = inputs
        adjoint = source + passed
        return (factor * adjoint, adjoint)

    initial = jnp.zeros(decays.shape[1:], jnp.float32)
    if backward:
        closing, values = lax.scan(retreat, initial, (decays, driving), reverse=True)
    else:
        closing, values = lax.scan(advance, initial, (decays, driving))
    return (values, closing)


def sweep_cols(decays, driving, backward):
    length = decays.shape[1]

    def advance(index, running):
        current, values = running
        place = length - 1 - index if backward else index
        place = jnp.asarray(place).astype(jnp.int32)
        factor = lax.dynamic_index_in_dim(decays, place, 1, keepdims=False)
        source = lax.dynamic_index_in_dim(driving, place, 1, keepdims=False)
        if backward:
            value = source + current
            values = lax.dynamic_update_index_in_dim(values, value, place, 1)
            current = factor * value
        else:
            current = factor * current + source
            values = lax.dynamic_update_index_in_dim(values, current, place, 1)
        return (current, values)

    initial = jnp.zeros(decays.shape[:1] + decays.shape[2:], jnp.float32)
    closing, values = lax.fori_loop(0, length, advance, (initial, jnp.zeros_like(driving)))
    return (values, closing)


def link_parts(final_state, exponent_sum, decay_rate):

    def combine(earlier, subsequent):
        return (earlier[0] * subsequent[0], subsequent[0] * earlier[1] + subsequent[1])

    products = jnp.exp(exponent_sum[:, None, :] * decay_rate)
    element = (products, final_state)
    identity = (jnp.ones_like(products), jnp.zeros_like(final_state))
    return (element, identity, combine)


def shards(features, step_size, write_weights, read_weights, decay_log, out_grad):
    highest = lax.Precision.HIGHEST
    decay_rate = -jnp.exp(decay_log)
    decays = jnp.exp(step_size[:, :, None, :] * decay_rate)
    driving = step_size[:, :, None, :] * write_weights[:, :, :, None] * features[:, :, None, :]
    running_rows = jnp.cumsum(step_size, 0)
    running_cols = jnp.cumsum(step_size, 1)
    sum_rows = running_rows[-1]
    sum_cols = running_cols[:, -1]
    local_rows, leaving_rows = sweep_rows(decays, driving, False)
    element, identity, combine = link_parts(leaving_rows, sum_rows, decay_rate)
    from_above = carried_in(element, "row", combine, identity, False)[1]
    vertical = local_rows + jnp.exp(running_rows[:, :, None, :] * decay_rate) * from_above[None]
    vert_prev = jnp.concatenate([from_above[None], vertical[:-1]], 0)
    local_cols, leaving_cols = sweep_cols(decays, vertical, False)
    element, identity, combine = link_parts(leaving_cols, sum_cols, decay_rate)
    from_left = carried_in(element, "col", combine, identity, False)[1]
    states = local_cols + jnp.exp(running_cols[:, :, None, :] * decay_rate) * from_left[:, None]
    states_prev = jnp.concatenate([from_left[:, None], states[:, :-1]], 1)
    direct = read_weights[:, :, :, None] * out_grad[:, :, None, :]
    adjoint_local, outgoing_cols = sweep_cols(decays, direct, True)
    element, identity, combine = link_parts(outgoing_cols, sum_cols, decay_rate)
    from_right = carried_in(element, "col", combine, identity, True)[1]
    after_cols = sum_cols[:, None, :] - running_cols
    adjoint_h = (
        adjoint_local + jnp.exp(after_cols[:, :, None, :] * decay_rate) * from_right[:, None]
    )
    adjoint_vlocal, outgoing_rows = sweep_rows(decays, adjoint_h, True)
    element, identity, combine = link_parts(outgoing_rows, sum_rows, decay_rate)
    from_below = carried_in(element, "row", combine, identity, True)[1]
    after_rows = sum_rows[None] - running_rows
    adjoint_v = adjoint_vlocal + jnp.exp(after_rows[:, :, None, :] * decay_rate) * from_below[None]
    exponent_grad = (adjoint_h * states_prev + adjoint_v * vert_prev) * decays
    through = jnp.einsum("hwnd,hwn->hwd", adjoint_v, write_weights, precision=highest)
    grad_features = step_size * through
    grad_step = features * through + jnp.einsum(
        "hwnd,nd->hwd", exponent_grad, decay_rate, precision=highest
    )
    grad_write = jnp.einsum("hwnd,hwd->hwn", adjoint_v, step_size * features, precision=highest)
    grad_read = jnp.einsum("hwnd,hwd->hwn", states, out_grad, precision=highest)
    partial_sum = jnp.einsum("hwnd,hwd->nd", exponent_grad, step_size, precision=highest)
    grad_decay = lax.psum(partial_sum, ("row", "col")) * decay_rate
    return (grad_features, grad_step, grad_write, grad_read, grad_decay)


def solution(mesh):
    in_specs = (
        P("row", "col", None),
        P("row", "col", None),
        P("row", "col", None),
        P("row", "col", None),
        P(),
        P("row", "col", None),
    )
    out_specs = (
        P("row", "col", None),
        P("row", "col", None),
        P("row", "col", None),
        P("row", "col", None),
        P(),
    )
    return jax.shard_map(shards, mesh=mesh, in_specs=in_specs, out_specs=out_specs, check_vma=False)
```

profile of v0, /device:TPU:1, one launch (start us, length us, event | category | flops | bytes accessed | tf_op | source)
XLA Modules:
  0.0 968.1 jit_solution(15481916507911445551)
XLA Ops:
  13.7 9.3 multiply_multiply_fusion
  23.0 5.8 copy-done
  28.8 6.2 copy.32
  35.0 7.9 broadcast.59.clone3
  42.9 79.4 %while.128 = (s32[]{:T(128)}, f32[64,16,128]{2,1,0:T(8,128)S(1)}, f32[32,64,16,128]{3,2,0,1:T(8,128)}, f32[32,64,16,128]{3,2,1,0:T(8,128)}, f32[32,64,16,128]{3,2,0,1:T(8,128)}, /*index=5*/s32[]{:T(128)}, s32[]{:T(128)}) while((s32[]{:T(128)}, f32[64,16,128]{2,1,0:T(8,128)S(1)}, f32[32,64,16,128]{3,2,0,1:T(8,128)}, ...), condition=%wide.region_11.12_spmd.clone, body=%wide.region_10.11_spmd.clone.sunk | while | flops 393219 | bytes 2622039 | solution.py:41
  42.9 2.5 bitcast_dynamic-update-slice_fusion.10
  45.4 2.5 bitcast_dynamic-update-slice_fusion.10
  47.9 2.5 bitcast_dynamic-update-slice_fusion.10
  50.4 2.5 bitcast_dynamic-update-slice_fusion.10
  52.9 2.5 bitcast_dynamic-update-slice_fusion.10
  57.9 2.5 bitcast_dynamic-update-slice_fusion.10
  60.4 2.5 bitcast_dynamic-update-slice_fusion.10
  62.8 2.5 bitcast_dynamic-update-slice_fusion.10
  65.3 2.5 bitcast_dynamic-update-slice_fusion.10
  67.8 2.5 bitcast_dynamic-update-slice_fusion.10
  70.3 2.5 bitcast_dynamic-update-slice_fusion.10
  82.6 2.5 bitcast_dynamic-update-slice_fusion.10
  90.1 2.5 bitcast_dynamic-update-slice_fusion.10
  95.0 2.5 bitcast_dynamic-update-slice_fusion.10
  97.5 2.5 bitcast_dynamic-update-slice_fusion.10
  109.9 2.5 bitcast_dynamic-update-slice_fusion.10
  119.8 2.5 bitcast_dynamic-update-slice_fusion.10
  123.2 4.0 fusion.18
  134.2 7.6 broadcast_multiply_fusion
  141.8 8.0 broadcast.59.clone3.2
  149.7 186.2 %while.124 = (s32[]{:T(128)}, f32[32,16,128]{2,1,0:T(8,128)S(1)}, f32[32,64,16,128]{3,2,0,1:T(8,128)}, f32[32,64,16,128]{3,2,0,1:T(8,128)}, f32[32,64,16,128]{3,...) while((s32[]{:T(128)}, f32[32,16,128]{2,1,0:T(8,128)S(1)}, ...), condition=%wide.region_1.2_spmd.clone, body=%wide.region_0.0_spmd.clone.sunk | while | flops 327687 | bytes 1835166 | solution.py:64
  338.5 13.5 %while.129 = (s32[]{:T(128)}, f32[64,16,128]{2,1,0:T(8,128)S(1)}, s32[]{:T(128)}, f32[8,64,16,128]{3,2,1,0:T(8,128)}, f32[8,64,16,128]{3,2,1,0:T(8,128)}, /*index=5*/s32[]{:T(128)}, s32[]{:T(128)}) while((s32[]{:T(128)}, f32[64,16,128]{2,1,0:T(8,128)S(1)}, s32[]{:T(128)}, f32[8,64,16,128]{3,2,1,0:T(8,128)}, ...), condition=%wide.region_13.14_spmd.clone, body=%wide.region_12.13_spmd.clone.sunk | while | flops 524292 | bytes 2097253 | solution.py:22
  352.0 12.2 %multiply_add_fusion.1 = f32[32,64,16,128]{3,2,0,1:T(8,128)} fusion(f32[32,64,16,128]{3,2,0,1:T(8,128)} %get-tuple-element.823, f32[64,16,128]{2,1,0:T(8,128)S(1)} %get-tuple-element.825, f32[32,64,128]{2,0,1:T(8,128)} %copy.41, f32[16,128]{1,0:T(8,128)S(1)} %exponential_negate_fusion), kind=kLoop, calls=%fused_computation.33 | loop fusion | flops 12582912 | bytes 35135488 | tf_op jit(solution)/shard_map/add | solution.py:91
  364.2 8.0 broadcast.59.clone3.1
  372.2 124.9 %while.130 = (s32[]{:T(128)}, f32[32,16,128]{2,1,0:T(8,128)S(1)}, f32[32,64,16,128]{3,2,0,1:T(8,128)}, f32[32,64,16,128]{3,2,0,1:T(8,128)}, f32[32,64,16,128]{3,2,0,1:T(8,128)}, /*index=5*/s32[]{:T(128)}, s32[]{:T(128)}) while((s32[]{:T(128)}, f32[32,16,128]{2,1,0:T(8,128)S(1)}, f32[32,64,16,128]{3,2,0,1:T(8,128)}, ...), condition=%wide.region_15.16_spmd.clone, body=%wide.region_14.15_spmd.clone.sunk | while | flops 196611 | bytes 1311319 | solution.py:64
  500.2 29.8 %while.125 = (s32[]{:T(128)}, f32[32,16,128]{2,1,0:T(8,128)}, s32[]{:T(128)}, f32[16,32,16,128]{3,2,1,0:T(8,128)}, f32[16,32,16,128]{3,2,1,0:T(8,128)}, /*index=5*/s32[]{:T(128)}, s32[]{:T(128)}, s32[]{:T(128)}, s32[]{:T(128)}) while((s32[]{:T(128)}, f32[32,16,128]{2,1,0:T(8,128)}, s32[]{:T(128)}, f32[16,32,16,128]{3,2,1,0:T(8,128)}, ...), condition=%wide.region_4.5_spmd.clone, body=%wide.region_3.4_spmd.clone.sunk | while | flops 262152 | bytes 1048739 | solution.py:22
  530.0 22.9 %all-gather.21.cloned.1.call-done = f32[512,16,128]{2,1,0:T(8,128)} async-done(((f32[32,16,128]{2,1,0:T(8,128)}), f32[512,16,128]{2,1,0:T(8,128)}) %all-gather.21.cloned.1.call-update) | async-done | bytes 4194320 | tf_op jit(solution)/shard_map/all_gather | solution.py:9
  552.9 20.3 %while.131 = (s32[]{:T(128)}, f32[32,16,128]{2,1,0:T(8,128)S(1)}, s32[]{:T(128)}, f32[16,32,16,128]{3,2,1,0:T(8,128)}, f32[16,32,16,128]{3,2,1,0:T(8,128)}, /*index=5*/s32[]{:T(128)}, s32[]{:T(128)}) while((s32[]{:T(128)}, f32[32,16,128]{2,1,0:T(8,128)S(1)}, s32[]{:T(128)}, f32[16,32,16,128]{3,2,1,0:T(8,128)}, ...), condition=%wide.region_17.18_spmd.clone, body=%wide.region_16.17_spmd.clone.sunk | while | flops 262148 | bytes 1048677 | solution.py:22
  573.2 23.2 %multiply_add_fusion = (f32[32,64,16,128]{3,2,0,1:T(8,128)}, f32[32,64,16,128]{3,2,0,1:T(8,128)}) fusion(f32[32,64,16,128]{3,2,0,1:T(8,128)} %get-tuple-element.828, f32[32,16,128]{2,1,0:T(8,128)S(1)} %get-tuple-element.827, f32[32,64,128]{2,0,1:T(8,128)} %copy-done.5, f32[16,128]{1,0:T(8,128)S(1)} %exponential_negate_fusion, ...), kind=kLoop, calls=%fused_computation.32 | loop fusion | flops 25165824 | bytes 69738496 | tf_op jit(solution)/shard_map/add | solution.py:96
  596.4 7.9 broadcast.59.clone2
  604.3 113.4 %while.126 = (s32[]{:T(128)}, f32[64,16,128]{2,1,0:T(8,128)S(1)}, f32[32,64,16,128]{3,2,0,1:T(8,128)}, f32[32,64,16,128]{3,2,1,0:T(8,128)}, f32[32,64,16,128]{3,...) while((s32[]{:T(128)}, f32[64,16,128]{2,1,0:T(8,128)S(1)}, f32[32,64,16,128]{3,2,0,1:T(8,128)}, ...), condition=%wide.region_6.7_spmd.clone, body=%wide.region_5.6_spmd.clone.sunk | while | flops 655364 | bytes 3670132 | solution.py:39
  721.8 2.9 copy.44
  724.7 11.6 %slice.19 = f32[31,64,16,128]{3,2,0,1:T(8,128)} slice(f32[32,64,16,128]{3,2,0,1:T(8,128)} %get-tuple-element.1542), slice={[0:31], [0:64], [0:16], [0:128]} | slice | bytes 32505856 | tf_op jit(solution)/shard_map/slice | solution.py:92
  736.3 13.9 %slice.18 = f32[32,63,16,128]{3,2,0,1:T(8,128)} slice(f32[32,64,16,128]{3,2,0,1:T(8,128)} %get-tuple-element.1087), slice={[0:32], [0:63], [0:16], [0:128]} | slice | bytes 33030144 | tf_op jit(solution)/shard_map/slice | solution.py:97
  753.5 27.6 %fusion.6 = f32[32,64,1,16]{3,2,1,0:T(1,128)} fusion(f32[32,64,128,1]{2,3,1,0:T(1,128)S(1)} %bitcast.158, f32[32,64,16,128]{3,2,0,1:T(8,128)S(1)} %bitcast.152), kind=kOutput, calls=%fused_computation.29 | convolution fusion | flops 50331648 | bytes 17956864 | tf_op jit(solution)/shard_map/hwnd,hwd->hwn/dot_general | solution.py:118
  781.1 2.9 copy.57
  784.1 13.5 %while.127 = (s32[]{:T(128)}, f32[64,16,128]{2,1,0:T(8,128)S(1)}, s32[]{:T(128)}, f32[8,64,16,128]{3,2,1,0:T(8,128)}, f32[8,64,16,128]{3,2,1,0:T(8,128)}, /*index=5*/s32[]{:T(128)}, s32[]{:T(128)}, s32[]{:T(128)}, s32[]{:T(128)}) while((s32[]{:T(128)}, f32[64,16,128]{2,1,0:T(8,128)S(1)}, s32[]{:T(128)}, ...), condition=%wide.region_9.10_spmd.clone, body=%wide.region_8.9_spmd.clone.sunk | while | flops 524296 | bytes 2097315 | solution.py:22
  797.6 34.8 %multiply_reduce_fusion = (f32[128,16]{0,1:T(8,128)S(1)}, f32[32,64,16,128]{3,2,0,1:T(8,128)}, f32[32,64,16,128]{3,2,0,1:T(8,128)}) fusion(f32[128,32,64]{0,1,2:T(8,128)} %copy.74, f32[16,128]{1,0:T(8,128)S(1)} %exponential_negate_fusion, f32[32,64,128]{2,0,1:T(8,128)S(1)} %copy-done.7, f32[31,64,16,128]{3,2,0,1:T(8,128)} %slice.19, ...), kind=kLoop, calls=%fused_computation.28 | loop fusion | flops 50329600 | bytes 104349696 | tf_op jit(solution)/shard_map/hwnd,hwd->nd/dot_general | solution.py:119
  832.3 64.6 %psum.7 = f32[16,128]{1,0:T(8,128)S(1)} all-reduce(f32[16,128]{1,0:T(8,128)S(1)} %bitcast.166), channel_id=1, replica_groups=mesh['row'=8,'col'=16] {'row','col'}, use_global_device_ids=true, to_apply=%region_18.19 | all-reduce | flops 2048 | bytes 16384 | tf_op jit(solution)/shard_map/psum | solution.py:120
  897.5 18.2 %fusion.10 = f32[32,64,1,128]{3,2,1,0:T(1,128)S(1)} fusion(f32[32,64,16,1]{2,3,1,0:T(1,128)} %copy.44, f32[32,64,16,128]{3,2,0,1:T(8,128)} %get-tuple-element.1079), kind=kOutput, calls=%fused_computation.40 | convolution fusion | flops 50331648 | bytes 17956864 | tf_op jit(solution)/shard_map/hwnd,hwn->hwd/dot_general | solution.py:112
  915.7 10.9 %multiply_reduce_fusion.1 = f32[128,32,64]{0,1,2:T(8,128)} fusion(f32[32,64,16,128]{3,2,0,1:T(8,128)} %get-tuple-element.1078, f32[128,16]{0,1:T(8,128)S(1)} %get-tuple-element.1086), kind=kLoop, calls=%fused_computation.31 | loop fusion | flops 8126464 | bytes 17833984
  926.6 3.6 fusion.17
  930.2 28.9 %fusion.8 = f32[32,64,1,16]{3,2,1,0:T(1,128)S(1)} fusion(f32[32,64,128,1]{2,3,1,0:T(1,128)S(1)} %bitcast.157, f32[32,64,16,128]{3,2,0,1:T(8,128)} %get-tuple-element.1079), kind=kOutput, calls=%fused_computation.38 | convolution fusion | flops 50331648 | bytes 17956864 | tf_op jit(solution)/shard_map/hwnd,hwd->hwn/dot_general | solution.py:117
  (394 shorter events, 565.5 us)
Async XLA Ops:
  7.2 331.3 %all-gather.19.cloned.1.call-start = ((), (), s32[]{:S(2)}) async-start(), calls=%async_computation.4 | async-start | bytes 4718592 | tf_op jit(solution)/shard_map/all_gather | solution.py:9
  9.8 13.2 %copy-start.6 = (f32[32,64,128]{2,0,1:T(8,128)}, f32[32,64,128]{2,0,1:T(8,128)S(1)}, u32[]{:S(2)}) copy-start(f32[32,64,128]{2,0,1:T(8,128)S(1)} %copy.27) | copy-start | bytes 3145732
  23.0 5.8 copy-start
  35.0 88.2 %copy-start.3 = (f32[32,64,128]{2,1,0:T(8,128)S(1)}, f32[32,64,128]{2,1,0:T(8,128)}, u32[]{:S(2)}) copy-start(f32[32,64,128]{2,1,0:T(8,128)} %param.23) | copy-start | bytes 3145732
  35.0 95.6 %copy-start.10 = (f32[32,64,16]{1,2,0:T(8,128)S(1)}, f32[32,64,16]{1,2,0:T(8,128)}, u32[]{:S(2)}) copy-start(f32[32,64,16]{1,2,0:T(8,128)} %param.25) | copy-start | bytes 393220
  122.3 0.8 copy-start.4
  123.1 215.4 %all-gather.13.cloned.1.call-start = ((), (), s32[]{:S(2)}) async-start(), calls=%async_computation.1 | async-start | bytes 4718592 | tf_op jit(solution)/shard_map/all_gather | solution.py:9
  128.1 372.1 %all-gather.11.cloned.1.call-start = ((), (), s32[]{:S(2)}) async-start(), calls=%async_computation | async-start | bytes 4456448 | tf_op jit(solution)/shard_map/all_gather | solution.py:9
  128.7 1.0 copy-start.5
  130.5 369.7 %all-gather.15.cloned.1.call-start = ((), (), s32[]{:S(2)}) async-start(), calls=%async_computation.2 | async-start | bytes 4456448 | tf_op jit(solution)/shard_map/all_gather | solution.py:9
  336.0 0.7 copy-start.2
  336.7 216.2 %all-gather.21.cloned.1.call-start = ((), (), s32[]{:S(2)}) async-start(), calls=%async_computation.5 | async-start | bytes 4456448 | tf_op jit(solution)/shard_map/all_gather | solution.py:9
  497.1 0.7 copy-start.8
  497.8 286.3 %all-gather.17.cloned.1.call-start = ((), (), s32[]{:S(2)}) async-start(), calls=%async_computation.3 | async-start | bytes 4718592 | tf_op jit(solution)/shard_map/all_gather | solution.py:9
  717.7 0.8 copy-start.1
  736.2 14.0 %slice-start = ((s8[16777216]{0:T(1024)(128)(4,1)}), s8[4194304]{0:T(1024)(128)(4,1)S(1)}, s32[]{:S(2)}) async-start(s8[16777216]{0:T(1024)(128)(4,1)} %bitcast.151), calls=%async_computation.6 | async-start | bytes 8388608
  736.2 14.0 %copy-start.9 = (f32[32,64,128]{2,1,0:T(8,128)S(1)}, f32[32,64,128]{2,1,0:T(8,128)}, u32[]{:S(2)}) copy-start(f32[32,64,128]{2,1,0:T(8,128)} %param.27) | copy-start | bytes 3145732
  736.2 14.6 %slice-start.1 = ((s8[16777216]{0:T(1024)(128)(4,1)}), s8[4194304]{0:T(1024)(128)(4,1)S(1)}, s32[]{:S(2)}) async-start(s8[16777216]{0:T(1024)(128)(4,1)} %bitcast.151), calls=%async_computation.7 | async-start | bytes 8388608
  736.3 16.1 %slice-start.2 = ((s8[16777216]{0:T(1024)(128)(4,1)}), s8[4194304]{0:T(1024)(128)(4,1)S(1)}, s32[]{:S(2)}) async-start(s8[16777216]{0:T(1024)(128)(4,1)} %bitcast.151), calls=%async_computation.8 | async-start | bytes 8388608
  736.3 17.2 %slice-start.3 = ((s8[16777216]{0:T(1024)(128)(4,1)}), s8[4194304]{0:T(1024)(128)(4,1)S(1)}, s32[]{:S(2)}) async-start(s8[16777216]{0:T(1024)(128)(4,1)} %bitcast.151), calls=%async_computation.9 | async-start | bytes 8388608
  753.5 44.0 %copy-start.7 = (f32[32,64,128]{2,0,1:T(8,128)S(1)}, f32[32,64,128]{2,0,1:T(8,128)}, u32[]{:S(2)}) copy-start(f32[32,64,128]{2,0,1:T(8,128)} %copy-done.6) | copy-start | bytes 3145732
  797.6 99.3 %copy-start.11 = (f32[16,128]{1,0:T(8,128)S(1)}, f32[16,128]{1,0:T(8,128)}, u32[]{:S(2)}) copy-start(f32[16,128]{1,0:T(8,128)} %param.26) | copy-start | bytes 24580
Sparse Core Ops, SparseCore 0:
  123.2 35.7 all-gather.18
  160.7 32.0 all-gather.12
  195.6 51.1 all-gather.10
  336.8 54.8 all-gather.14
  497.9 54.8 all-gather.20
  718.6 32.1 all-gather.16
where the time goes:
time: 984 us; the launch traced here: 968 us
  other arithmetic  690 us (70%)
  local copies, waits for them, and re-layouts  98.4 us (10%)
  matrix products  74.7 us (8%)
  blocking collectives  64.6 us (7%)
  waiting for transfers between devices  23 us (2%)
  between operations  14.6 us (1%)
    dynamic_update_slice x64, other arithmetic, sweep_rows(): closing, values = lax.scan(advance, initial, (decays, driving))  143 us
    dynamic_update_slice x64, other arithmetic, advance(): values = lax.dynamic_update_index_in_dim(values, current, place, 1)  125 us
    dynamic_update_slice x64, other arithmetic, advance(): values = lax.dynamic_update_index_in_dim(values, value, place, 1)  108 us
    mul x64, other arithmetic, advance(): current = factor * value  76.4 us
    select_n x48, other arithmetic, lap(): return jax.tree.map(lambda a, b: jnp.where(reached, a, b), new, before)  76.4 us
    psum x1, blocking collectives, shards(): grad_decay = lax.psum(partial_sum, ('row', 'col')) * decay_rate  64.6 us
    mul x32, other arithmetic, retreat(): return (factor * adjoint, adjoint)  49.2 us
    dot_general x1, other arithmetic, shards(): jnp.einsum('hwnd,hwd->nd', exponent_grad, step_size, precision=highest)  34.8 us
  transfers between devices with their start and end apart: 6, of which 1 were waited for; matrix products, arithmetic and copies ran while one was open for 48% of the time, Pallas kernels for 0%

commit v1 on v0

--- a/solution.py
+++ b/solution.py
@@ -117,7 +117,7 @@
     grad_write = jnp.einsum("hwnd,hwd->hwn", adjoint_v, step_size * features, precision=highest)
     grad_read = jnp.einsum("hwnd,hwd->hwn", states, out_grad, precision=highest)
     partial_sum = jnp.einsum("hwnd,hwd->nd", exponent_grad, step_size, precision=highest)
-    grad_decay = lax.psum(partial_sum, ("row", "col")) * decay_rate
+    grad_decay = lax.psum(lax.psum(partial_sum, "row"), "col") * decay_rate
     return (grad_features, grad_step, grad_write, grad_read, grad_decay)
 
 

time: 984 us -> 973 us (0.989)
  the two profiles are of different devices: /device:TPU:1 before, /device:TPU:0 now
where the time goes in v1:
time: 973 us; the launch traced here: 957 us
  other arithmetic  690 us (71%)
  local copies, waits for them, and re-layouts  98.5 us (10%)
  matrix products  74.7 us (8%)
  blocking collectives  53.8 us (6%)
  waiting for transfers between devices  22.3 us (2%)
  between operations  14.6 us (2%)
    dynamic_update_slice x64, other arithmetic, sweep_rows(): closing, values = lax.scan(advance, initial, (decays, driving))  143 us
    dynamic_update_slice x64, other arithmetic, advance(): values = lax.dynamic_update_index_in_dim(values, current, place, 1)  125 us
    dynamic_update_slice x64, other arithmetic, advance(): values = lax.dynamic_update_index_in_dim(values, value, place, 1)  109 us
    select_n x48, other arithmetic, lap(): return jax.tree.map(lambda a, b: jnp.where(reached, a, b), new, before)  76.3 us
    mul x64, other arithmetic, advance(): current = factor * value  76.3 us
    psum x2, blocking collectives, shards(): grad_decay = lax.psum(lax.psum(partial_sum, 'row'), 'col') * decay_rate  53.8 us
    mul x32, other arithmetic, retreat(): return (factor * adjoint, adjoint)  49.2 us
    dot_general x1, other arithmetic, shards(): jnp.einsum('hwnd,hwd->nd', exponent_grad, step_size, precision=highest)  34.8 us
  transfers between devices with their start and end apart: 6, of which 1 were waited for; matrix products, arithmetic and copies ran while one was open for 49% of the time, Pallas kernels for 0%

profile of v1, /device:TPU:0, one launch (start us, length us, event | category | flops | bytes accessed | tf_op | source)
XLA Modules:
  0.0 957.4 jit_solution(5432978173219175599)
XLA Ops:
  13.7 9.3 multiply_multiply_fusion
  23.0 5.8 copy-done
  28.8 6.2 copy.32
  35.0 7.9 broadcast.59.clone3
  42.9 79.4 %while.128 = (s32[]{:T(128)}, f32[64,16,128]{2,1,0:T(8,128)S(1)}, f32[32,64,16,128]{3,2,0,1:T(8,128)}, f32[32,64,16,128]{3,2,1,0:T(8,128)}, f32[32,64,16,128]{3,2,0,1:T(8,128)}, /*index=5*/s32[]{:T(128)}, s32[]{:T(128)}) while((s32[]{:T(128)}, f32[64,16,128]{2,1,0:T(8,128)S(1)}, f32[32,64,16,128]{3,2,0,1:T(8,128)}, ...), condition=%wide.region_11.12_spmd.clone, body=%wide.region_10.11_spmd.clone.sunk | while | flops 393219 | bytes 2622039 | solution.py:41
  45.4 2.5 bitcast_dynamic-update-slice_fusion.10
  55.2 2.5 bitcast_dynamic-update-slice_fusion.10
  57.7 2.5 bitcast_dynamic-update-slice_fusion.10
  60.2 2.5 bitcast_dynamic-update-slice_fusion.10
  62.7 2.5 bitcast_dynamic-update-slice_fusion.10
  65.2 2.5 bitcast_dynamic-update-slice_fusion.10
  67.7 2.5 bitcast_dynamic-update-slice_fusion.10
  72.7 2.5 bitcast_dynamic-update-slice_fusion.10
  75.2 2.5 bitcast_dynamic-update-slice_fusion.10
  77.7 2.5 bitcast_dynamic-update-slice_fusion.10
  82.6 2.5 bitcast_dynamic-update-slice_fusion.10
  85.1 2.5 bitcast_dynamic-update-slice_fusion.10
  97.5 2.5 bitcast_dynamic-update-slice_fusion.10
  104.9 2.5 bitcast_dynamic-update-slice_fusion.10
  109.9 2.5 bitcast_dynamic-update-slice_fusion.10
  112.4 2.5 bitcast_dynamic-update-slice_fusion.10
  123.2 4.0 fusion.18
  134.2 7.6 broadcast_multiply_fusion
  141.8 8.0 broadcast.59.clone3.2
  149.8 186.4 %while.124 = (s32[]{:T(128)}, f32[32,16,128]{2,1,0:T(8,128)S(1)}, f32[32,64,16,128]{3,2,0,1:T(8,128)}, f32[32,64,16,128]{3,2,0,1:T(8,128)}, f32[32,64,16,128]{3,...) while((s32[]{:T(128)}, f32[32,16,128]{2,1,0:T(8,128)S(1)}, ...), condition=%wide.region_1.2_spmd.clone, body=%wide.region_0.0_spmd.clone.sunk | while | flops 327687 | bytes 1835166 | solution.py:64
  338.8 13.4 %while.129 = (s32[]{:T(128)}, f32[64,16,128]{2,1,0:T(8,128)S(1)}, s32[]{:T(128)}, f32[8,64,16,128]{3,2,1,0:T(8,128)}, f32[8,64,16,128]{3,2,1,0:T(8,128)}, /*index=5*/s32[]{:T(128)}, s32[]{:T(128)}) while((s32[]{:T(128)}, f32[64,16,128]{2,1,0:T(8,128)S(1)}, s32[]{:T(128)}, f32[8,64,16,128]{3,2,1,0:T(8,128)}, ...), condition=%wide.region_13.14_spmd.clone, body=%wide.region_12.13_spmd.clone.sunk | while | flops 524292 | bytes 2097253 | solution.py:22
  352.2 12.2 %multiply_add_fusion.1 = f32[32,64,16,128]{3,2,0,1:T(8,128)} fusion(f32[32,64,16,128]{3,2,0,1:T(8,128)} %get-tuple-element.823, f32[64,16,128]{2,1,0:T(8,128)S(1)} %get-tuple-element.825, f32[32,64,128]{2,0,1:T(8,128)} %copy.41, f32[16,128]{1,0:T(8,128)S(1)} %exponential_negate_fusion), kind=kLoop, calls=%fused_computation.33 | loop fusion | flops 12582912 | bytes 35135488 | tf_op jit(solution)/shard_map/add | solution.py:91
  364.5 8.0 broadcast.59.clone3.1
  372.4 125.2 %while.130 = (s32[]{:T(128)}, f32[32,16,128]{2,1,0:T(8,128)S(1)}, f32[32,64,16,128]{3,2,0,1:T(8,128)}, f32[32,64,16,128]{3,2,0,1:T(8,128)}, f32[32,64,16,128]{3,2,0,1:T(8,128)}, /*index=5*/s32[]{:T(128)}, s32[]{:T(128)}) while((s32[]{:T(128)}, f32[32,16,128]{2,1,0:T(8,128)S(1)}, f32[32,64,16,128]{3,2,0,1:T(8,128)}, ...), condition=%wide.region_15.16_spmd.clone, body=%wide.region_14.15_spmd.clone.sunk | while | flops 196611 | bytes 1311319 | solution.py:64
  500.8 29.8 %while.125 = (s32[]{:T(128)}, f32[32,16,128]{2,1,0:T(8,128)}, s32[]{:T(128)}, f32[16,32,16,128]{3,2,1,0:T(8,128)}, f32[16,32,16,128]{3,2,1,0:T(8,128)}, /*index=5*/s32[]{:T(128)}, s32[]{:T(128)}, s32[]{:T(128)}, s32[]{:T(128)}) while((s32[]{:T(128)}, f32[32,16,128]{2,1,0:T(8,128)}, s32[]{:T(128)}, f32[16,32,16,128]{3,2,1,0:T(8,128)}, ...), condition=%wide.region_4.5_spmd.clone, body=%wide.region_3.4_spmd.clone.sunk | while | flops 262152 | bytes 1048739 | solution.py:22
  530.5 22.2 %all-gather.21.cloned.1.call-done = f32[512,16,128]{2,1,0:T(8,128)} async-done(((f32[32,16,128]{2,1,0:T(8,128)}), f32[512,16,128]{2,1,0:T(8,128)}) %all-gather.21.cloned.1.call-update) | async-done | bytes 4194320 | tf_op jit(solution)/shard_map/all_gather | solution.py:9
  552.8 20.3 %while.131 = (s32[]{:T(128)}, f32[32,16,128]{2,1,0:T(8,128)S(1)}, s32[]{:T(128)}, f32[16,32,16,128]{3,2,1,0:T(8,128)}, f32[16,32,16,128]{3,2,1,0:T(8,128)}, /*index=5*/s32[]{:T(128)}, s32[]{:T(128)}) while((s32[]{:T(128)}, f32[32,16,128]{2,1,0:T(8,128)S(1)}, s32[]{:T(128)}, f32[16,32,16,128]{3,2,1,0:T(8,128)}, ...), condition=%wide.region_17.18_spmd.clone, body=%wide.region_16.17_spmd.clone.sunk | while | flops 262148 | bytes 1048677 | solution.py:22
  573.1 23.3 %multiply_add_fusion = (f32[32,64,16,128]{3,2,0,1:T(8,128)}, f32[32,64,16,128]{3,2,0,1:T(8,128)}) fusion(f32[32,64,16,128]{3,2,0,1:T(8,128)} %get-tuple-element.828, f32[32,16,128]{2,1,0:T(8,128)S(1)} %get-tuple-element.827, f32[32,64,128]{2,0,1:T(8,128)} %copy-done.5, f32[16,128]{1,0:T(8,128)S(1)} %exponential_negate_fusion, ...), kind=kLoop, calls=%fused_computation.32 | loop fusion | flops 25165824 | bytes 69738496 | tf_op jit(solution)/shard_map/add | solution.py:96
  596.4 7.9 broadcast.59.clone2
  604.3 113.4 %while.126 = (s32[]{:T(128)}, f32[64,16,128]{2,1,0:T(8,128)S(1)}, f32[32,64,16,128]{3,2,0,1:T(8,128)}, f32[32,64,16,128]{3,2,1,0:T(8,128)}, f32[32,64,16,128]{3,...) while((s32[]{:T(128)}, f32[64,16,128]{2,1,0:T(8,128)S(1)}, f32[32,64,16,128]{3,2,0,1:T(8,128)}, ...), condition=%wide.region_6.7_spmd.clone, body=%wide.region_5.6_spmd.clone.sunk | while | flops 655364 | bytes 3670132 | solution.py:39
  721.8 2.9 copy.44
  724.7 11.6 %slice.19 = f32[31,64,16,128]{3,2,0,1:T(8,128)} slice(f32[32,64,16,128]{3,2,0,1:T(8,128)} %get-tuple-element.1542), slice={[0:31], [0:64], [0:16], [0:128]} | slice | bytes 32505856 | tf_op jit(solution)/shard_map/slice | solution.py:92
  736.3 13.9 %slice.18 = f32[32,63,16,128]{3,2,0,1:T(8,128)} slice(f32[32,64,16,128]{3,2,0,1:T(8,128)} %get-tuple-element.1087), slice={[0:32], [0:63], [0:16], [0:128]} | slice | bytes 33030144 | tf_op jit(solution)/shard_map/slice | solution.py:97
  753.6 27.6 %fusion.6 = f32[32,64,1,16]{3,2,1,0:T(1,128)} fusion(f32[32,64,128,1]{2,3,1,0:T(1,128)S(1)} %bitcast.158, f32[32,64,16,128]{3,2,0,1:T(8,128)S(1)} %bitcast.152), kind=kOutput, calls=%fused_computation.29 | convolution fusion | flops 50331648 | bytes 17956864 | tf_op jit(solution)/shard_map/hwnd,hwd->hwn/dot_general | solution.py:118
  781.2 2.9 copy.57
  784.1 13.5 %while.127 = (s32[]{:T(128)}, f32[64,16,128]{2,1,0:T(8,128)S(1)}, s32[]{:T(128)}, f32[8,64,16,128]{3,2,1,0:T(8,128)}, f32[8,64,16,128]{3,2,1,0:T(8,128)}, /*index=5*/s32[]{:T(128)}, s32[]{:T(128)}, s32[]{:T(128)}, s32[]{:T(128)}) while((s32[]{:T(128)}, f32[64,16,128]{2,1,0:T(8,128)S(1)}, s32[]{:T(128)}, ...), condition=%wide.region_9.10_spmd.clone, body=%wide.region_8.9_spmd.clone.sunk | while | flops 524296 | bytes 2097315 | solution.py:22
  797.6 34.8 %multiply_reduce_fusion = (f32[128,16]{0,1:T(8,128)S(1)}, f32[32,64,16,128]{3,2,0,1:T(8,128)}, f32[32,64,16,128]{3,2,0,1:T(8,128)}) fusion(f32[128,32,64]{0,1,2:T(8,128)} %copy.74, f32[16,128]{1,0:T(8,128)S(1)} %exponential_negate_fusion, f32[32,64,128]{2,0,1:T(8,128)S(1)} %copy-done.7, f32[31,64,16,128]{3,2,0,1:T(8,128)} %slice.19, ...), kind=kLoop, calls=%fused_computation.28 | loop fusion | flops 50329600 | bytes 104349696 | tf_op jit(solution)/shard_map/hwnd,hwd->nd/dot_general | solution.py:119
  832.4 14.7 %psum.14 = f32[16,128]{1,0:T(8,128)S(1)} all-reduce(f32[16,128]{1,0:T(8,128)S(1)} %bitcast.166), channel_id=1, replica_groups=mesh['row'=8,'col'=16] {'row'}, use_global_device_ids=true, to_apply=%region_18.19 | all-reduce | flops 2048 | bytes 16384 | tf_op jit(solution)/shard_map/psum | solution.py:120
  847.2 39.0 %psum.15 = f32[16,128]{1,0:T(8,128)S(1)} all-reduce(f32[16,128]{1,0:T(8,128)S(1)} %psum.14), channel_id=1, replica_groups=mesh['row'=8,'col'=16] {'col'}, use_global_device_ids=true, to_apply=%region_19.20 | all-reduce | flops 2048 | bytes 16384 | tf_op jit(solution)/shard_map/psum | solution.py:120
  886.8 18.2 %fusion.10 = f32[32,64,1,128]{3,2,1,0:T(1,128)S(1)} fusion(f32[32,64,16,1]{2,3,1,0:T(1,128)} %copy.44, f32[32,64,16,128]{3,2,0,1:T(8,128)} %get-tuple-element.1079), kind=kOutput, calls=%fused_computation.40 | convolution fusion | flops 50331648 | bytes 17956864 | tf_op jit(solution)/shard_map/hwnd,hwn->hwd/dot_general | solution.py:112
  905.0 10.9 %multiply_reduce_fusion.1 = f32[128,32,64]{0,1,2:T(8,128)} fusion(f32[32,64,16,128]{3,2,0,1:T(8,128)} %get-tuple-element.1078, f32[128,16]{0,1:T(8,128)S(1)} %get-tuple-element.1086), kind=kLoop, calls=%fused_computation.31 | loop fusion | flops 8126464 | bytes 17833984
  915.9 3.6 fusion.17
  919.6 28.9 %fusion.8 = f32[32,64,1,16]{3,2,1,0:T(1,128)S(1)} fusion(f32[32,64,128,1]{2,3,1,0:T(1,128)S(1)} %bitcast.157, f32[32,64,16,128]{3,2,0,1:T(8,128)} %get-tuple-element.1079), kind=kOutput, calls=%fused_computation.38 | convolution fusion | flops 50331648 | bytes 17956864 | tf_op jit(solution)/shard_map/hwnd,hwd->hwn/dot_general | solution.py:117
  (395 shorter events, 568.5 us)
Async XLA Ops:
  7.2 331.6 %all-gather.19.cloned.1.call-start = ((), (), s32[]{:S(2)}) async-start(), calls=%async_computation.4 | async-start | bytes 4718592 | tf_op jit(solution)/shard_map/all_gather | solution.py:9
  9.8 13.2 %copy-start.6 = (f32[32,64,128]{2,0,1:T(8,128)}, f32[32,64,128]{2,0,1:T(8,128)S(1)}, u32[]{:S(2)}) copy-start(f32[32,64,128]{2,0,1:T(8,128)S(1)} %copy.27) | copy-start | bytes 3145732
  23.0 5.8 copy-start
  35.0 88.2 %copy-start.3 = (f32[32,64,128]{2,1,0:T(8,128)S(1)}, f32[32,64,128]{2,1,0:T(8,128)}, u32[]{:S(2)}) copy-start(f32[32,64,128]{2,1,0:T(8,128)} %param.23) | copy-start | bytes 3145732
  35.0 95.6 %copy-start.10 = (f32[32,64,16]{1,2,0:T(8,128)S(1)}, f32[32,64,16]{1,2,0:T(8,128)}, u32[]{:S(2)}) copy-start(f32[32,64,16]{1,2,0:T(8,128)} %param.25) | copy-start | bytes 393220
  122.3 0.8 copy-start.4
  123.1 215.6 %all-gather.13.cloned.1.call-start = ((), (), s32[]{:S(2)}) async-start(), calls=%async_computation.1 | async-start | bytes 4718592 | tf_op jit(solution)/shard_map/all_gather | solution.py:9
  128.1 372.7 %all-gather.11.cloned.1.call-start = ((), (), s32[]{:S(2)}) async-start(), calls=%async_computation | async-start | bytes 4456448 | tf_op jit(solution)/shard_map/all_gather | solution.py:9
  128.7 1.0 copy-start.5
  130.5 370.2 %all-gather.15.cloned.1.call-start = ((), (), s32[]{:S(2)}) async-start(), calls=%async_computation.2 | async-start | bytes 4456448 | tf_op jit(solution)/shard_map/all_gather | solution.py:9
  336.2 0.7 copy-start.2
  336.9 215.8 %all-gather.21.cloned.1.call-start = ((), (), s32[]{:S(2)}) async-start(), calls=%async_computation.5 | async-start | bytes 4456448 | tf_op jit(solution)/shard_map/all_gather | solution.py:9
  497.7 0.7 copy-start.8
  498.4 285.8 %all-gather.17.cloned.1.call-start = ((), (), s32[]{:S(2)}) async-start(), calls=%async_computation.3 | async-start | bytes 4718592 | tf_op jit(solution)/shard_map/all_gather | solution.py:9
  717.7 0.8 copy-start.1
  736.3 14.0 %slice-start = ((s8[16777216]{0:T(1024)(128)(4,1)}), s8[4194304]{0:T(1024)(128)(4,1)S(1)}, s32[]{:S(2)}) async-start(s8[16777216]{0:T(1024)(128)(4,1)} %bitcast.151), calls=%async_computation.6 | async-start | bytes 8388608
  736.3 14.0 %copy-start.9 = (f32[32,64,128]{2,1,0:T(8,128)S(1)}, f32[32,64,128]{2,1,0:T(8,128)}, u32[]{:S(2)}) copy-start(f32[32,64,128]{2,1,0:T(8,128)} %param.27) | copy-start | bytes 3145732
  736.3 14.7 %slice-start.1 = ((s8[16777216]{0:T(1024)(128)(4,1)}), s8[4194304]{0:T(1024)(128)(4,1)S(1)}, s32[]{:S(2)}) async-start(s8[16777216]{0:T(1024)(128)(4,1)} %bitcast.151), calls=%async_computation.7 | async-start | bytes 8388608
  736.3 16.1 %slice-start.2 = ((s8[16777216]{0:T(1024)(128)(4,1)}), s8[4194304]{0:T(1024)(128)(4,1)S(1)}, s32[]{:S(2)}) async-start(s8[16777216]{0:T(1024)(128)(4,1)} %bitcast.151), calls=%async_computation.8 | async-start | bytes 8388608
  736.3 17.3 %slice-start.3 = ((s8[16777216]{0:T(1024)(128)(4,1)}), s8[4194304]{0:T(1024)(128)(4,1)S(1)}, s32[]{:S(2)}) async-start(s8[16777216]{0:T(1024)(128)(4,1)} %bitcast.151), calls=%async_computation.9 | async-start | bytes 8388608
  753.6 44.0 %copy-start.7 = (f32[32,64,128]{2,0,1:T(8,128)S(1)}, f32[32,64,128]{2,0,1:T(8,128)}, u32[]{:S(2)}) copy-start(f32[32,64,128]{2,0,1:T(8,128)} %copy-done.6) | copy-start | bytes 3145732
  797.6 88.6 %copy-start.11 = (f32[16,128]{1,0:T(8,128)S(1)}, f32[16,128]{1,0:T(8,128)}, u32[]{:S(2)}) copy-start(f32[16,128]{1,0:T(8,128)} %param.26) | copy-start | bytes 24580
Sparse Core Ops, SparseCore 0:
  123.2 34.5 all-gather.18
  159.6 32.0 all-gather.12
  194.4 51.5 all-gather.10
  337.1 54.1 all-gather.14
  498.5 54.2 all-gather.20
  718.6 31.6 all-gather.16
